TPU v7x, 32 devices: a whole 2x2x4 slice. The times are simulated.
32 devices in a mesh: rows: 16 (over z, y, core), heads: 2 (over x).
Axes of the slice: x: 2, y: 2, z: 4, core: 2. Of those that a mesh axis runs over, the one named last changes fastest.
Arguments:
- features: bfloat16 [8192, 1664], P(('rows', 'heads')), may hold values from -6 to 6
- segment_ids: int32 [8192], P(('rows', 'heads')), may hold values from 0 to 1, as said below
- padding_mask: int32 [8192], P(('rows', 'heads')), may hold values from 0 to 1, as said below
- w_proj: bfloat16 [1664, 1024], replicated, may hold values from -0.15625 to 0.15625
- proj_bias: float32 [1024], replicated, may hold values from -3 to 3
- gain_attn: float32 [1024], replicated, may hold values from 0.1 to 1.9
- w_qkv: bfloat16 [1024, 3, 1024], P(None, None, 'heads'), may hold values from -0.09375 to 0.09375
- w_out: bfloat16 [1024, 1024], P('heads'), may hold values from -3 to 3
- gain_ffn: float32 [1024], replicated, may hold values from 0.1 to 1.9
- w_gate_up: bfloat16 [1024, 2, 2816], P(None, None, 'heads'), may hold values from -0.1875 to 0.1875
- w_down: bfloat16 [2816, 1024], P('heads'), may hold values from -0.109375 to 0.109375
- cotangent: bfloat16 [8192, 1024], P(('rows', 'heads')), may hold values from -6 to 6
Outputs:
- layer_out: bfloat16 [8192, 1024], P(('rows', 'heads'))
- grad_features: float32 [8192, 1664], P(('rows', 'heads'))
- grad_proj: float32 [1664, 1024], replicated
- grad_bias: float32 [1024], replicated
- grad_gain_attn: float32 [1024], replicated
- grad_qkv: float32 [1024, 3, 1024], P(None, None, 'heads')
- grad_out: float32 [1024, 1024], P('heads')
- grad_gain_ffn: float32 [1024], replicated
- grad_gate_up: float32 [1024, 2, 2816], P(None, None, 'heads')
- grad_down: float32 [2816, 1024], P('heads')
Inputs may be any that keep to these rules, and one draw needn't show every extreme that they name: `segment_ids`: within each aligned block of 512 tokens (one packed row) the ids start at 0 and never fall; each pair holds 256 patches followed by its text, and the padding at a row's end has one id of its own. `padding_mask`: in each packed row the ones form a leading run that ends where the row's last whole pair ends; the rest is 0.
All inputs are finite; a program needn't handle non-finite values.
Results may differ from a plain program's by a relative error of at most 0.024.
Values may be sent and summed in bfloat16 or wider, within the bound.
No kernel may reach another device: no remote copies, remote signals or barrier semaphores. Data moves between devices by JAX's collectives and lax.ppermute only.
A program may use at most 128 MiB of HBM per device.

v0:
```python
import jax
import jax.numpy as jnp
from jax import lax
from jax.sharding import PartitionSpec as P

HEAD_DIM = 64
LEN_MAX = 2048
EPSILON = 1e-06
MASKED = -1000000000.0


def gelu_tanh(values):
    return jax.nn.gelu(values, approximate=True)


def contract(left, right, left_dim, right_dim):
    return lax.dot_general(
        left, right, (((left_dim,), (right_dim,)), ((), ())), preferred_element_type=jnp.float32
    )


def rms_forward(values, gain):
    scale = lax.rsqrt(jnp.mean(values * values, axis=-1, keepdims=True) + EPSILON)
    return (values * scale * gain, scale)


def rms_backward(values, scale, gain, grad_normed):
    unit = values * scale
    grad_unit = grad_normed * gain
    grad_values = scale * (grad_unit - unit * jnp.mean(grad_unit * unit, axis=-1, keepdims=True))
    return (grad_values, jnp.sum(grad_normed * unit, axis=0))


def block_scores(
    queries, key_rows, segments, padding, query_start, row_start, query_count, seq_len
):
    query_block = lax.dynamic_slice_in_dim(queries, query_start, query_count, 0)
    scores = jnp.einsum("qhd,khd->hqk", query_block, key_rows, preferred_element_type=jnp.float32)
    query_segment = lax.dynamic_slice_in_dim(segments, query_start, query_count, 0)
    query_place = query_start + jnp.arange(query_count)
    key_place = row_start + jnp.arange(seq_len)
    allowed = (query_segment[:, None] == segments[None, :]) & (
        (padding[None, :] == 1) | (query_place[:, None] == key_place[None, :])
    )
    return (jnp.where(allowed[None], scores, MASKED), query_block, key_rows)


def attention_forward(queries, key_rows, value_rows, segments, padding, seq_len, query_count):
    group_tokens = queries.shape[0]
    per_seq = seq_len // query_count

    def one_block(number):
        query_start = number * query_count
        row_start = number // per_seq * seq_len
        scores, _, _ = block_scores(
            queries, key_rows, segments, padding, query_start, row_start, query_count, seq_len
        )
        top = jnp.max(scores, axis=-1, keepdims=True)
        expo = jnp.exp(scores - top)
        weight_sum = jnp.sum(expo, axis=-1, keepdims=True)
        probs = (expo / weight_sum).astype(jnp.bfloat16)
        mixed = jnp.einsum("hqk,khd->qhd", probs, value_rows, preferred_element_type=jnp.float32)
        return (mixed.astype(jnp.bfloat16), (top + jnp.log(weight_sum))[:, :, 0])

    mixed, log_sums = lax.map(one_block, jnp.arange(group_tokens // query_count))
    return (mixed.reshape(group_tokens, -1), log_sums)


def attention_backward(
    queries, key_rows, value_rows, segments, padding, log_sums, grad_mixed, seq_len, query_count
):
    group_tokens, heads_here, head_size = queries.shape
    per_seq = seq_len // query_count

    def one_block(carry, item):
        grad_keys, grad_values = carry
        number, log_sum = item
        query_start = number * query_count
        row_start = number // per_seq * seq_len
        scores, query_block, key_block = block_scores(
            queries, key_rows, segments, padding, query_start, row_start, query_count, seq_len
        )
        grad_block = lax.dynamic_slice_in_dim(grad_mixed, query_start, query_count, 0)
        probs = jnp.exp(scores - log_sum[:, :, None])
        grad_probs = jnp.einsum(
            "qhd,khd->hqk", grad_block, value_rows, preferred_element_type=jnp.float32
        )
        grad_scores = probs * (grad_probs - jnp.sum(grad_probs * probs, axis=-1, keepdims=True))
        grad_scores = grad_scores.astype(jnp.bfloat16)
        grad_query = jnp.einsum(
            "hqk,khd->qhd", grad_scores, key_block, preferred_element_type=jnp.float32
        )
        key_part = jnp.einsum(
            "hqk,qhd->khd", grad_scores, query_block, preferred_element_type=jnp.float32
        )
        value_part = jnp.einsum(
            "hqk,qhd->khd",
            probs.astype(jnp.bfloat16),
            grad_block,
            preferred_element_type=jnp.float32,
        )
        grad_keys = grad_keys + key_part
        grad_values = grad_values + value_part
        return ((grad_keys, grad_values), grad_query)

    zero_grads = jnp.zeros((group_tokens, heads_here, head_size), jnp.float32)
    (grad_keys, grad_values), grad_queries = lax.scan(
        one_block, (zero_grads, zero_grads), (jnp.arange(group_tokens // query_count), log_sums)
    )
    return (grad_queries.reshape(group_tokens, heads_here, head_size), grad_keys, grad_values)


def local(
    features,
    segment_ids,
    padding_mask,
    w_proj,
    proj_bias,
    gain_attn,
    w_qkv,
    w_out,
    gain_ffn,
    w_gate_up,
    w_down,
    cotangent,
):
    local_tokens = features.shape[0]
    model_width = w_proj.shape[1]
    attn_cols = w_qkv.shape[2]
    heads_here = attn_cols // HEAD_DIM
    group_tokens = local_tokens * lax.axis_size("heads")
    seq_len = min(LEN_MAX, group_tokens)
    query_count = min(512, seq_len)
    qkv_flat = w_qkv.reshape(model_width, 3 * attn_cols)
    lifted = jnp.dot(features, w_proj, preferred_element_type=jnp.float32) + proj_bias
    normed, scale_attn = rms_forward(lifted, gain_attn)
    gathered, segments, padding = (
        lax.all_gather(normed.astype(jnp.bfloat16), "heads", axis=0, tiled=True),
        lax.all_gather(segment_ids, "heads", axis=0, tiled=True),
        lax.all_gather(padding_mask, "heads", axis=0, tiled=True),
    )
    projected = jnp.dot(gathered, qkv_flat, preferred_element_type=jnp.float32).astype(jnp.bfloat16)
    projected = projected.reshape(group_tokens, 3, heads_here, HEAD_DIM)
    queries, key_rows, value_rows = (projected[:, 0], projected[:, 1], projected[:, 2])
    mixed, log_sums = attention_forward(
        queries, key_rows, value_rows, segments, padding, seq_len, query_count
    )
    middle = lifted + lax.psum_scatter(
        jnp.dot(mixed, w_out, preferred_element_type=jnp.float32).astype(jnp.bfloat16),
        "heads",
        scatter_dimension=0,
        tiled=True,
    ).astype(jnp.float32)
    normed_ffn, scale_ffn = rms_forward(middle, gain_ffn)
    normed_ffn_b = normed_ffn.astype(jnp.bfloat16)
    ff_here = w_gate_up.shape[2]
    gathered_ffn = lax.all_gather(normed_ffn_b, "heads", axis=0, tiled=True)
    gate_flat = w_gate_up.reshape(model_width, 2 * ff_here)
    gate_up = jnp.dot(gathered_ffn, gate_flat, preferred_element_type=jnp.float32)
    activ, gelu_pull = jax.vjp(gelu_tanh, gate_up[:, :ff_here])
    up_part = gate_up[:, ff_here:]
    hidden = (activ * up_part).astype(jnp.bfloat16)
    layer_out = middle + lax.psum_scatter(
        jnp.dot(hidden, w_down, preferred_element_type=jnp.float32).astype(jnp.bfloat16),
        "heads",
        scatter_dimension=0,
        tiled=True,
    ).astype(jnp.float32)
    grad_gathered = lax.all_gather(cotangent, "heads", axis=0, tiled=True)
    grad_hidden = contract(grad_gathered, w_down, 1, 1)
    grad_pre = jnp.concatenate(
        [gelu_pull(grad_hidden * up_part)[0], grad_hidden * activ], axis=1
    ).astype(jnp.bfloat16)
    grad_gu_local = contract(gathered_ffn, grad_pre, 0, 0).reshape(model_width, 2, ff_here)
    grad_down_local = contract(hidden, grad_gathered, 0, 0)
    grad_normed_ffn = lax.psum_scatter(
        contract(grad_pre, gate_flat, 1, 1).astype(jnp.bfloat16),
        "heads",
        scatter_dimension=0,
        tiled=True,
    ).astype(jnp.float32)
    grad_gate_up, grad_down = (
        lax.psum(grad_gu_local.astype(jnp.bfloat16), "rows").astype(jnp.float32),
        lax.psum(grad_down_local.astype(jnp.bfloat16), "rows").astype(jnp.float32),
    )
    grad_ffn_norm, grad_gain_ffn = rms_backward(middle, scale_ffn, gain_ffn, grad_normed_ffn)
    grad_middle = cotangent.astype(jnp.float32) + grad_ffn_norm
    grad_mid_b = grad_middle.astype(jnp.bfloat16)
    grad_attn_in = lax.all_gather(grad_mid_b, "heads", axis=0, tiled=True)
    grad_mixed = contract(grad_attn_in, w_out, 1, 1).astype(jnp.bfloat16)
    grad_out_local = contract(mixed, grad_attn_in, 0, 0)
    grad_queries, grad_keys, grad_values = attention_backward(
        queries,
        key_rows,
        value_rows,
        segments,
        padding,
        log_sums,
        grad_mixed.reshape(group_tokens, heads_here, HEAD_DIM),
        seq_len,
        query_count,
    )
    grad_heads = (
        jnp.stack([grad_queries, grad_keys, grad_values], axis=1)
        .astype(jnp.bfloat16)
        .reshape(group_tokens, 3 * attn_cols)
    )
    grad_qkv_local = contract(gathered, grad_heads, 0, 0).reshape(model_width, 3, attn_cols)
    grad_normed = lax.psum_scatter(
        contract(grad_heads, qkv_flat, 1, 1).astype(jnp.bfloat16),
        "heads",
        scatter_dimension=0,
        tiled=True,
    ).astype(jnp.float32)
    grad_qkv, grad_out = (
        lax.psum(grad_qkv_local.astype(jnp.bfloat16), "rows").astype(jnp.float32),
        lax.psum(grad_out_local.astype(jnp.bfloat16), "rows").astype(jnp.float32),
    )
    grad_attn_norm, grad_gain_attn = rms_backward(lifted, scale_attn, gain_attn, grad_normed)
    grad_lifted = grad_middle + grad_attn_norm
    grad_lift_b = grad_lifted.astype(jnp.bfloat16)
    grad_features = contract(grad_lift_b, w_proj, 1, 1)
    grad_proj_local = contract(features, grad_lift_b, 0, 0)
    grad_proj, grad_bias, grad_gain_attn, grad_gain_ffn = lax.psum(
        (grad_proj_local, jnp.sum(grad_lifted, axis=0), grad_gain_attn, grad_gain_ffn),
        ("rows", "heads"),
    )
    return (
        layer_out.astype(jnp.bfloat16),
        grad_features,
        grad_proj,
        grad_bias,
        grad_gain_attn,
        grad_qkv,
        grad_out,
        grad_gain_ffn,
        grad_gate_up,
        grad_down,
    )


def solution(mesh):
    in_specs = (
        P(("rows", "heads"), None),
        P(("rows", "heads")),
        P(("rows", "heads")),
        P(),
        P(),
        P(),
        P(None, None, "heads"),
        P("heads", None),
        P(),
        P(None, None, "heads"),
        P("heads", None),
        P(("rows", "heads"), None),
    )
    out_specs = (
        P(("rows", "heads"), None),
        P(("rows", "heads"), None),
        P(),
        P(),
        P(),
        P(None, None, "heads"),
        P("heads", None),
        P(),
        P(None, None, "heads"),
        P("heads", None),
    )
    return jax.shard_map(local, mesh=mesh, in_specs=in_specs, out_specs=out_specs, check_vma=False)
```

profile of v0, /device:TPU:0, one launch (start us, length us, event | category | flops | bytes accessed | tf_op | source)
XLA Modules:
  0.0 693.1 jit_solution(15542330360389667371)
XLA Ops:
  13.5 5.1 all-gather.1
  18.7 4.7 copy.39
  23.4 4.3 all-gather
  28.6 9.0 %all-gather.7.cloned.1.call-done = bf16[512,1024]{1,0:T(8,128)(2,1)} async-done(((bf16[256,1024]{1,0:T(8,128)(2,1)}), bf16[512,1024]{1,0:T(8,128)(2,1)}) %all-gather.7.cloned.1.call-update) | async-done | bytes 1048592 | tf_op jit(solution)/shard_map/all_gather | solution.py:138
  37.6 5.2 convolution_convert_fusion.2
  51.5 3.4 fusion.20
  57.5 20.4 %reduce-scatter.5.cloned.1.call-done = bf16[256,1024]{1,0:T(8,128)(2,1)} async-done(((bf16[512,1024]{1,0:T(8,128)(2,1)}), bf16[256,1024]{1,0:T(8,128)(2,1)}) %reduce-scatter.5.cloned.1.call-update) | async-done | bytes 524304 | tf_op jit(solution)/shard_map/reduce_scatter | solution.py:148
  83.0 6.2 copy.53
  89.1 14.2 %all-gather.9.cloned.1.call-done = bf16[512,1024]{1,0:T(8,128)(2,1)} async-done(((bf16[256,1024]{1,0:T(8,128)(2,1)}), bf16[512,1024]{1,0:T(8,128)(2,1)}) %all-gather.9.cloned.1.call-update) | async-done | bytes 1048592 | tf_op jit(solution)/shard_map/all_gather | solution.py:157
  103.3 8.7 %fusion.48 = f32[512,2816]{1,0:T(8,128)} fusion(bf16[512,1024]{1,0:T(8,128)(2,1)} %all-gather.9.cloned.1.call-done, bf16[1024,2816]{1,0:T(8,128)(2,1)} %bitcast.92), kind=kOutput, calls=%fused_computation.90 | convolution fusion | flops 2952790016 | bytes 12582912 | tf_op jit(solution)/shard_map/dot_general | solution.py:159
  112.0 14.2 %all-gather.11.cloned.1.call-done = bf16[512,1024]{1,0:T(8,128)(2,1)} async-done(((bf16[256,1024]{1,0:T(8,128)(2,1)}), bf16[512,1024]{1,0:T(8,128)(2,1)}) %all-gather.11.cloned.1.call-update) | async-done | bytes 1048592 | tf_op jit(solution)/shard_map/all_gather | solution.py:169
  126.1 8.8 %fusion.14 = (bf16[512,1408]{1,0:T(8,128)(2,1)S(1)}, bf16[512,1408]{1,0:T(8,128)(2,1)S(1)}, bf16[512,1408]{1,0:T(8,128)(2,1)}) fusion(f32[512,2816]{1,0:T(8,128)} %fusion.48, bf16[512,1024]{1,0:T(8,128)(2,1)} %all-gather.11.cloned.1.call-done, bf16[1408,1024]{1,0:T(8,128)(2,1)} %param.22), kind=kOutput, calls=%fused_computation.26 | convolution fusion | flops 1495138304 | bytes 14024704 | tf_op jit(solution)/shard_map/dot_general | solution.py:17
  136.5 4.1 fusion.16
  140.7 20.4 %reduce-scatter.9.cloned.1.call-done = bf16[256,1024]{1,0:T(8,128)(2,1)} async-done(((bf16[512,1024]{1,0:T(8,128)(2,1)}), bf16[256,1024]{1,0:T(8,128)(2,1)}) %reduce-scatter.9.cloned.1.call-update) | async-done | bytes 524304 | tf_op jit(solution)/shard_map/reduce_scatter | solution.py:176
  166.3 21.2 %all-gather.13.cloned.1.call-done = bf16[512,1024]{1,0:T(8,128)(2,1)} async-done(((bf16[256,1024]{1,0:T(8,128)(2,1)}), bf16[512,1024]{1,0:T(8,128)(2,1)}) %all-gather.13.cloned.1.call-update) | async-done | bytes 1048592 | tf_op jit(solution)/shard_map/all_gather | solution.py:189
  189.9 5.5 fusion.17
  195.4 5.2 multiply_reduce_fusion
  210.8 5.0 convolution_convert_fusion.5
  215.9 15.3 %reduce-scatter.11.cloned.1.call-done = bf16[256,1024]{1,0:T(8,128)(2,1)} async-done(((bf16[512,1024]{1,0:T(8,128)(2,1)}), bf16[256,1024]{1,0:T(8,128)(2,1)}) %reduce-scatter.11.cloned.1.call-update) | async-done | bytes 524304 | tf_op jit(solution)/shard_map/reduce_scatter | solution.py:209
  233.1 21.4 %reduce-scatter.7.cloned.1.call-done = bf16[256,1024]{1,0:T(8,128)(2,1)} async-done(((bf16[512,1024]{1,0:T(8,128)(2,1)}), bf16[256,1024]{1,0:T(8,128)(2,1)}) %reduce-scatter.7.cloned.1.call-update) | async-done | bytes 524304 | tf_op jit(solution)/shard_map/reduce_scatter | solution.py:163
  254.5 3.6 fusion.46
  258.8 4.0 convolution_bitcast_fusion
  263.2 7.9 %convolution_convert_fusion = bf16[1024,2816]{1,0:T(8,128)(2,1)} fusion(bf16[512,1024]{1,0:T(8,128)(2,1)} %all-gather.9.cloned.1.call-done, bf16[512,1408]{1,0:T(8,128)(2,1)} %copy-done.24, bf16[512,1408]{1,0:T(8,128)(2,1)} %copy-done.23), kind=kOutput, calls=%fused_computation.7 | convolution fusion | flops 2961440768 | bytes 9699328 | tf_op jit(solution)/shard_map/dot_general | solution.py:17
  271.0 12.1 %convert_element_type.141 = bf16[1024,2,1408]{2,1,0:T(2,128)(2,1)} reshape(bf16[1024,2816]{1,0:T(8,128)(2,1)} %convolution_convert_fusion) | data formatting | bytes 11534336 | tf_op jit(solution)/shard_map/convert_element_type | solution.py:183
  283.2 5.1 convolution_convert_fusion.1
  290.2 3.5 convolution_convert_fusion.3
  293.8 40.2 %all-reduce = (f32[1024]{0:T(1024)}, f32[1024]{0:T(1024)}, f32[1024]{0:T(1024)}) all-reduce(f32[1024]{0:T(1024)S(1)} %get-tuple-element.108, f32[1024]{0:T(1024)S(1)} %get-tuple-element.99, f32[1024]{0:T(1024)S(1)} %get-tuple-element.97), channel_id=1, replica_groups=mesh['rows'=16,'heads'=2] {'rows','heads'}, use_global_device_ids=true, to_apply=%region_13.14 | all-reduce | flops 3072 | bytes 24576 | tf_op jit(solution)/shard_map/psum | solution.py:224
  337.4 86.7 %all-reduce.5.cloned.1.call-done = f32[1664,1024]{0,1:T(8,128)} async-done(((f32[1664,1024]{0,1:T(8,128)}), f32[1664,1024]{0,1:T(8,128)}) %all-reduce.5.cloned.1.call-update) | async-done | bytes 6815760 | tf_op jit(solution)/shard_map/psum | solution.py:224
  424.1 7.6 %copy.46 = f32[1664,1024]{1,0:T(8,128)} copy(f32[1664,1024]{0,1:T(8,128)} %all-reduce.5.cloned.1.call-done) | data formatting | bytes 13631488
  431.7 238.1 %all-reduce.7.cloned.1.call-done = (bf16[1024,3,512]{2,0,1:T(8,128)(2,1)}, bf16[512,1024]{1,0:T(8,128)(2,1)}, bf16[1024,2,1408]{2,1,0:T(2,128)(2,1)}, bf16[1408,1024]{1,0:T(8,128)(2,1)}) async-done(((bf16[1024,3,512]{2,0,1:T(8,128)(2,1)}, bf16[512,1024]{1,0:T(8,128)(2,1)}, bf16[1024,2,1408]{2,1,0:T(2,128)(2,1)}, bf16[1408,1024]{1,0:T(8,128)(2,1)}), (bf16[1024,3,512]{2,0,1:T(8,128)(2,1)}, ...) | async-done | bytes 12845072 | tf_op jit(solution)/shard_map/psum | solution.py:216
  669.9 5.6 convert_element_type.137
  677.1 5.7 convert_element_type.142
  (109 shorter events, 55.8 us)
Async XLA Ops:
  7.2 2.0 copy-start
  7.2 5.3 copy-start.15
  7.2 6.3 copy-start.16
  7.2 30.4 %all-gather.7.cloned.1.call-start = ((), (), s32[]{:S(2)}) async-start(), calls=%async_computation.4 | async-start | bytes 1572864 | tf_op jit(solution)/shard_map/all_gather | solution.py:138
  13.5 64.4 %reduce-scatter.5.cloned.1.call-start = ((), (), s32[]{:S(2)}) async-start(), calls=%async_computation.5 | async-start | bytes 1572864 | tf_op jit(solution)/shard_map/reduce_scatter | solution.py:148
  18.7 4.7 copy-start.17
  45.4 2.7 copy-start.4
  48.1 3.4 copy-start.1
  51.5 4.2 copy-start.18
  54.9 24.6 %copy-start.14 = (f32[1024]{0:T(1024)S(1)}, f32[1024]{0:T(1024)}, u32[]{:S(2)}) copy-start(f32[1024]{0:T(1024)} %param.20) | copy-start | bytes 12292
  57.4 45.9 %all-gather.9.cloned.1.call-start = ((), (), s32[]{:S(2)}) async-start(), calls=%async_computation.6 | async-start | bytes 1572864 | tf_op jit(solution)/shard_map/all_gather | solution.py:157
  81.9 44.3 %all-gather.11.cloned.1.call-start = ((), (), s32[]{:S(2)}) async-start(), calls=%async_computation.8 | async-start | bytes 1572864 | tf_op jit(solution)/shard_map/all_gather | solution.py:169
  82.4 78.7 %reduce-scatter.9.cloned.1.call-start = ((), (), s32[]{:S(2)}) async-start(), calls=%async_computation.9 | async-start | bytes 1572864 | tf_op jit(solution)/shard_map/reduce_scatter | solution.py:176
  126.1 10.4 %copy-start.6 = (bf16[128,8,2,1408]{3,1,2,0:T(8,128)(2,1)S(1)}, bf16[128,8,2,1408]{3,1,2,0:T(8,128)(2,1)}, u32[]{:S(2)}) copy-start(bf16[128,8,2,1408]{3,1,2,0:T(8,128)(2,1)} %copy.53) | copy-start | bytes 17301508
  140.7 46.9 %all-gather.13.cloned.1.call-start = ((), (), s32[]{:S(2)}) async-start(), calls=%async_computation.10 | async-start | bytes 1572864 | tf_op jit(solution)/shard_map/all_gather | solution.py:189
  166.1 65.1 %reduce-scatter.11.cloned.1.call-start = ((), (), s32[]{:S(2)}) async-start(), calls=%async_computation.11 | async-start | bytes 1572864 | tf_op jit(solution)/shard_map/reduce_scatter | solution.py:209
  187.5 2.3 copy-start.5
  189.9 5.5 copy-start.3
  189.9 10.7 %slice-start = ((s8[8388608]{0:T(1024)(128)(4,1)}), s8[4194304]{0:T(1024)(128)(4,1)S(1)}, s32[]{:S(2)}) async-start(s8[8388608]{0:T(1024)(128)(4,1)} %bitcast.82), calls=%async_computation.14 | async-start | bytes 8388608
  195.4 5.2 slice-start.1
  205.5 2.5 copy-start.7
  210.7 43.7 %reduce-scatter.7.cloned.1.call-start = ((), (), s32[]{:S(2)}) async-start(), calls=%async_computation.7 | async-start | bytes 1572864 | tf_op jit(solution)/shard_map/reduce_scatter | solution.py:163
  215.8 208.3 %all-reduce.5.cloned.1.call-start = ((), (), s32[]{:S(2)}) async-start(), calls=%async_computation.12 | async-start | bytes 13631488 | tf_op jit(solution)/shard_map/psum | solution.py:224
  254.5 4.4 copy-start.13
  262.9 406.9 %all-reduce.7.cloned.1.call-start = ((), (), s32[]{:S(2)}) async-start(), calls=%async_computation.13 | async-start | bytes 25690112 | tf_op jit(solution)/shard_map/psum | solution.py:216
  283.1 5.1 copy-start.20
  283.1 5.1 copy-start.22
  288.3 1.9 copy-start.19
  669.9 7.2 %slice-start.2 = ((s8[5767168]{0:T(1024)(128)(4,1)}), s8[4194304]{0:T(1024)(128)(4,1)S(1)}, s32[]{:S(2)}) async-start(s8[5767168]{0:T(1024)(128)(4,1)} %bitcast.90), calls=%async_computation.16 | async-start | bytes 8388608
  669.9 5.7 copy-start.12
  669.9 7.2 %slice-start.3 = ((s8[5767168]{0:T(1024)(128)(4,1)}), s8[1572864]{0:T(1024)(128)(4,1)S(1)}, s32[]{:S(2)}) async-start(s8[5767168]{0:T(1024)(128)(4,1)} %bitcast.90), calls=%async_computation.17 | async-start | bytes 3145728
  677.1 5.8 copy-start.8
  (7 other events, 8.2 us)
Sparse Core Ops, SparseCore 0:
  13.6 23.9 all-gather.6
  57.6 20.3 reduce-scatter.4
  82.0 21.3 all-gather.8
  104.8 21.2 all-gather.10
  140.8 20.3 reduce-scatter.8
  166.2 21.2 all-gather.12
  210.9 20.3 reduce-scatter.10
  234.1 20.3 reduce-scatter.6
  263.0 161.0 all-reduce.4
  429.7 240.1 all-reduce.6
where the time goes:
time: 701 us; the launch traced here: 693 us
  waiting for transfers between devices  462 us (66%)
  matrix products  85.5 us (12%)
  blocking collectives  49.6 us (7%)
  local copies, waits for them, and re-layouts  43.6 us (6%)
  other arithmetic  36.7 us (5%)
  between operations  14.7 us (2%)
    psum x1, waiting for transfers between devices, local(): lax.psum(grad_qkv_local.astype(jnp.bfloat16), 'rows').astype(jnp.float32)  238 us
    psum x1, waiting for transfers between devices, local(): lax.psum((grad_proj_local, jnp.sum(grad_lifted, axis=0), grad_gain_attn,...  86.7 us
    dot_general x10, matrix products, contract(): lax.dot_general(left, right, (((left_dim,), (right_dim,)), ((), ())), pre...  43.7 us
    psum x1, blocking collectives, local(): lax.psum((grad_proj_local, jnp.sum(grad_lifted, axis=0), grad_gain_attn,...  40.2 us
    unnamed x61, local copies, waits for them, and re-layouts  28.9 us
    reduce_scatter x1, waiting for transfers between devices, local(): lax.psum_scatter(jnp.dot(hidden, w_down, preferred_element_type=jnp.float...  21.4 us
    all_gather x1, waiting for transfers between devices, local(): grad_attn_in = lax.all_gather(grad_mid_b, 'heads', axis=0, tiled=True)  21.2 us
    reduce_scatter x1, waiting for transfers between devices, local(): lax.psum_scatter(jnp.dot(mixed, w_out, preferred_element_type=jnp.float32...  20.4 us
  transfers between devices with their start and end apart: 10, of which 10 were waited for; matrix products, arithmetic and copies ran while one was open for 10% of the time, Pallas kernels for 0%

commit v1 on v0

--- a/solution.py
+++ b/solution.py
@@ -222,8 +222,10 @@
     grad_features = contract(grad_lift_b, w_proj, 1, 1)
     grad_proj_local = contract(features, grad_lift_b, 0, 0)
     grad_proj, grad_bias, grad_gain_attn, grad_gain_ffn = lax.psum(
-        (grad_proj_local, jnp.sum(grad_lifted, axis=0), grad_gain_attn, grad_gain_ffn),
-        ("rows", "heads"),
+        lax.psum(
+            (grad_proj_local, jnp.sum(grad_lifted, axis=0), grad_gain_attn, grad_gain_ffn), "heads"
+        ),
+        "rows",
     )
     return (
         layer_out.astype(jnp.bfloat16),

time: 701 us -> 847 us (1.21)
  waiting for transfers between devices: 462 us -> 579 us
  blocking collectives: 49.6 us -> 79.2 us
    psum x0 -> x1, waiting for transfers between devices: none -> 134 us  [local(): lax.psum(lax.psum((grad_proj_local, jnp.sum(grad_lifted, axis=0), grad_ga...]
    psum x1, waiting for transfers between devices: 238 us -> 174 us  [local(): lax.psum(grad_qkv_local.astype(jnp.bfloat16), 'rows').astype(jnp.float32)]
    psum x0 -> x1, blocking collectives: none -> 62.9 us  [local(): lax.psum(lax.psum((grad_proj_local, jnp.sum(grad_lifted, axis=0), grad_ga...]
    psum x1, waiting for transfers between devices: 86.7 us -> 134 us  [local(): lax.psum((grad_proj_local, jnp.sum(grad_lifted, axis=0), grad_gain_attn,...]
    psum x1, blocking collectives: 40.2 us -> 6.91 us  [local(): lax.psum((grad_proj_local, jnp.sum(grad_lifted, axis=0), grad_gain_attn,...]
  transfers between devices with their start and end apart: 10 -> 11, of which waited for: 10 -> 11; matrix products, arithmetic and copies ran while one was open for 10% -> 9% of each run, Pallas kernels for 0% -> 0%
where the time goes in v1:
time: 847 us; the launch traced here: 840 us
  waiting for transfers between devices  579 us (68%)
  matrix products  85.5 us (10%)
  blocking collectives  79.2 us (9%)
  local copies, waits for them, and re-layouts  43.5 us (5%)
  other arithmetic  36.7 us (4%)
  between operations  14.4 us (2%)
    psum x1, waiting for transfers between devices, local(): lax.psum(grad_qkv_local.astype(jnp.bfloat16), 'rows').astype(jnp.float32)  174 us
    psum x1, waiting for transfers between devices, local(): lax.psum(lax.psum((grad_proj_local, jnp.sum(grad_lifted, axis=0), grad_ga...  134 us
    psum x1, waiting for transfers between devices, local(): lax.psum((grad_proj_local, jnp.sum(grad_lifted, axis=0), grad_gain_attn,...  134 us
    psum x1, blocking collectives, local(): lax.psum(lax.psum((grad_proj_local, jnp.sum(grad_lifted, axis=0), grad_ga...  62.9 us
    dot_general x10, matrix products, contract(): lax.dot_general(left, right, (((left_dim,), (right_dim,)), ((), ())), pre...  43.6 us
    unnamed x61, local copies, waits for them, and re-layouts  28.8 us
    reduce_scatter x1, waiting for transfers between devices, local(): lax.psum_scatter(jnp.dot(hidden, w_down, preferred_element_type=jnp.float...  21.4 us
    all_gather x1, waiting for transfers between devices, local(): grad_attn_in = lax.all_gather(grad_mid_b, 'heads', axis=0, tiled=True)  21.2 us
  transfers between devices with their start and end apart: 11, of which 11 were waited for; matrix products, arithmetic and copies ran while one was open for 9% of the time, Pallas kernels for 0%

profile of v1, /device:TPU:0, one launch (start us, length us, event | category | flops | bytes accessed | tf_op | source)
XLA Modules:
  0.0 839.7 jit_solution(10721050488910317960)
XLA Ops:
  13.5 5.1 all-gather.1
  18.7 4.7 copy.39
  23.4 4.3 all-gather
  28.6 9.0 %all-gather.7.cloned.1.call-done = bf16[512,1024]{1,0:T(8,128)(2,1)} async-done(((bf16[256,1024]{1,0:T(8,128)(2,1)}), bf16[512,1024]{1,0:T(8,128)(2,1)}) %all-gather.7.cloned.1.call-update) | async-done | bytes 1048592 | tf_op jit(solution)/shard_map/all_gather | solution.py:138
  37.6 5.2 convolution_convert_fusion.2
  57.5 20.4 %reduce-scatter.5.cloned.1.call-done = bf16[256,1024]{1,0:T(8,128)(2,1)} async-done(((bf16[512,1024]{1,0:T(8,128)(2,1)}), bf16[256,1024]{1,0:T(8,128)(2,1)}) %reduce-scatter.5.cloned.1.call-update) | async-done | bytes 524304 | tf_op jit(solution)/shard_map/reduce_scatter | solution.py:148
  83.0 6.2 copy.53
  89.1 14.2 %all-gather.9.cloned.1.call-done = bf16[512,1024]{1,0:T(8,128)(2,1)} async-done(((bf16[256,1024]{1,0:T(8,128)(2,1)}), bf16[512,1024]{1,0:T(8,128)(2,1)}) %all-gather.9.cloned.1.call-update) | async-done | bytes 1048592 | tf_op jit(solution)/shard_map/all_gather | solution.py:157
  103.4 8.7 %fusion.48 = f32[512,2816]{1,0:T(8,128)} fusion(bf16[512,1024]{1,0:T(8,128)(2,1)} %all-gather.9.cloned.1.call-done, bf16[1024,2816]{1,0:T(8,128)(2,1)} %bitcast.92), kind=kOutput, calls=%fused_computation.90 | convolution fusion | flops 2952790016 | bytes 12582912 | tf_op jit(solution)/shard_map/dot_general | solution.py:159
  112.0 14.2 %all-gather.11.cloned.1.call-done = bf16[512,1024]{1,0:T(8,128)(2,1)} async-done(((bf16[256,1024]{1,0:T(8,128)(2,1)}), bf16[512,1024]{1,0:T(8,128)(2,1)}) %all-gather.11.cloned.1.call-update) | async-done | bytes 1048592 | tf_op jit(solution)/shard_map/all_gather | solution.py:169
  126.2 8.8 %fusion.14 = (bf16[512,1408]{1,0:T(8,128)(2,1)S(1)}, bf16[512,1408]{1,0:T(8,128)(2,1)S(1)}, bf16[512,1408]{1,0:T(8,128)(2,1)}) fusion(f32[512,2816]{1,0:T(8,128)} %fusion.48, bf16[512,1024]{1,0:T(8,128)(2,1)} %all-gather.11.cloned.1.call-done, bf16[1408,1024]{1,0:T(8,128)(2,1)} %param.22), kind=kOutput, calls=%fused_computation.26 | convolution fusion | flops 1495138304 | bytes 14024704 | tf_op jit(solution)/shard_map/dot_general | solution.py:17
  136.6 4.1 fusion.16
  140.8 20.4 %reduce-scatter.9.cloned.1.call-done = bf16[256,1024]{1,0:T(8,128)(2,1)} async-done(((bf16[512,1024]{1,0:T(8,128)(2,1)}), bf16[256,1024]{1,0:T(8,128)(2,1)}) %reduce-scatter.9.cloned.1.call-update) | async-done | bytes 524304 | tf_op jit(solution)/shard_map/reduce_scatter | solution.py:176
  166.3 21.2 %all-gather.13.cloned.1.call-done = bf16[512,1024]{1,0:T(8,128)(2,1)} async-done(((bf16[256,1024]{1,0:T(8,128)(2,1)}), bf16[512,1024]{1,0:T(8,128)(2,1)}) %all-gather.13.cloned.1.call-update) | async-done | bytes 1048592 | tf_op jit(solution)/shard_map/all_gather | solution.py:189
  189.9 5.5 fusion.17
  195.4 5.2 multiply_reduce_fusion
  210.8 5.0 convolution_convert_fusion.5
  215.9 15.3 %reduce-scatter.11.cloned.1.call-done = bf16[256,1024]{1,0:T(8,128)(2,1)} async-done(((bf16[512,1024]{1,0:T(8,128)(2,1)}), bf16[256,1024]{1,0:T(8,128)(2,1)}) %reduce-scatter.11.cloned.1.call-update) | async-done | bytes 524304 | tf_op jit(solution)/shard_map/reduce_scatter | solution.py:209
  233.1 21.4 %reduce-scatter.7.cloned.1.call-done = bf16[256,1024]{1,0:T(8,128)(2,1)} async-done(((bf16[512,1024]{1,0:T(8,128)(2,1)}), bf16[256,1024]{1,0:T(8,128)(2,1)}) %reduce-scatter.7.cloned.1.call-update) | async-done | bytes 524304 | tf_op jit(solution)/shard_map/reduce_scatter | solution.py:163
  254.5 3.6 fusion.46
  258.9 4.0 convolution_bitcast_fusion
  263.2 7.9 convolution_convert_fusion
  271.1 12.1 %convert_element_type.141 = bf16[1024,2,1408]{2,1,0:T(2,128)(2,1)} reshape(bf16[1024,2816]{1,0:T(8,128)(2,1)} %convolution_convert_fusion) | data formatting | bytes 11534336 | tf_op jit(solution)/shard_map/convert_element_type | solution.py:183
  283.2 5.0 convolution_convert_fusion.1
  293.6 134.0 %all-reduce.7.cloned.1.call-done = f32[1664,1024]{0,1:T(8,128)} async-done(((f32[1664,1024]{0,1:T(8,128)}), f32[1664,1024]{0,1:T(8,128)}) %all-reduce.7.cloned.1.call-update) | async-done | bytes 6815760 | tf_op jit(solution)/shard_map/psum | solution.py:225
  427.7 6.9 all-reduce.1
  434.6 62.9 %all-reduce = (f32[1024]{0:T(1024)}, f32[1024]{0:T(1024)}, f32[1024]{0:T(1024)}) all-reduce(f32[1024]{0:T(1024)S(1)} %get-tuple-element.104, f32[1024]{0:T(1024)S(1)} %get-tuple-element.105, f32[1024]{0:T(1024)S(1)} %get-tuple-element.106), channel_id=1, replica_groups=mesh['rows'=16,'heads'=2] {'rows'}, use_global_device_ids=true, to_apply=%region_15.16 | all-reduce | flops 3072 | bytes 24576 | tf_op jit(solution)/shard_map/psum | solution.py:224
  500.8 173.8 %all-reduce.11.cloned.1.call-done = (bf16[1024,3,512]{2,0,1:T(8,128)(2,1)}, bf16[512,1024]{1,0:T(8,128)(2,1)}, bf16[1024,2,1408]{2,1,0:T(2,128)(2,1)}, bf16[1408,1024]{1,0:T(8,128)(2,1)}) async-done(((bf16[1024,3,512]{2,0,1:T(8,128)(2,1)}, bf16[512,1024]{1,0:T(8,128)(2,1)}, bf16[1024,2,1408]{2,1,0:T(2,128)(2,1)}, bf16[1408,1024]{1,0:T(8,128)(2,1)}), (bf16[1024,3,512]{2,0,1:T(8,128)(2,1)}, ...) | async-done | bytes 12845072 | tf_op jit(solution)/shard_map/psum | solution.py:216
  674.7 5.6 convert_element_type.137
  681.9 5.7 convert_element_type.142
  690.9 134.4 %all-reduce.9.cloned.1.call-done = f32[1664,1024]{0,1:T(8,128)} async-done(((f32[1664,1024]{0,1:T(8,128)}), f32[1664,1024]{0,1:T(8,128)}) %all-reduce.9.cloned.1.call-update) | async-done | bytes 6815760 | tf_op jit(solution)/shard_map/psum | solution.py:224
  825.4 7.6 copy.46
  (113 shorter events, 62.7 us)
Async XLA Ops:
  7.2 2.0 copy-start
  7.2 5.3 copy-start.15
  7.2 6.3 copy-start.16
  7.2 30.4 %all-gather.7.cloned.1.call-start = ((), (), s32[]{:S(2)}) async-start(), calls=%async_computation.4 | async-start | bytes 1572864 | tf_op jit(solution)/shard_map/all_gather | solution.py:138
  13.5 64.5 %reduce-scatter.5.cloned.1.call-start = ((), (), s32[]{:S(2)}) async-start(), calls=%async_computation.5 | async-start | bytes 1572864 | tf_op jit(solution)/shard_map/reduce_scatter | solution.py:148
  18.7 4.7 copy-start.17
  45.4 2.7 copy-start.4
  48.1 3.4 copy-start.1
  51.5 4.2 copy-start.18
  55.0 24.6 %copy-start.14 = (f32[1024]{0:T(1024)S(1)}, f32[1024]{0:T(1024)}, u32[]{:S(2)}) copy-start(f32[1024]{0:T(1024)} %param.20) | copy-start | bytes 12292
  57.5 45.9 %all-gather.9.cloned.1.call-start = ((), (), s32[]{:S(2)}) async-start(), calls=%async_computation.6 | async-start | bytes 1572864 | tf_op jit(solution)/shard_map/all_gather | solution.py:157
  81.9 44.3 %all-gather.11.cloned.1.call-start = ((), (), s32[]{:S(2)}) async-start(), calls=%async_computation.8 | async-start | bytes 1572864 | tf_op jit(solution)/shard_map/all_gather | solution.py:169
  82.5 78.7 %reduce-scatter.9.cloned.1.call-start = ((), (), s32[]{:S(2)}) async-start(), calls=%async_computation.9 | async-start | bytes 1572864 | tf_op jit(solution)/shard_map/reduce_scatter | solution.py:176
  126.2 10.4 %copy-start.6 = (bf16[128,8,2,1408]{3,1,2,0:T(8,128)(2,1)S(1)}, bf16[128,8,2,1408]{3,1,2,0:T(8,128)(2,1)}, u32[]{:S(2)}) copy-start(bf16[128,8,2,1408]{3,1,2,0:T(8,128)(2,1)} %copy.53) | copy-start | bytes 17301508
  140.7 46.8 %all-gather.13.cloned.1.call-start = ((), (), s32[]{:S(2)}) async-start(), calls=%async_computation.10 | async-start | bytes 1572864 | tf_op jit(solution)/shard_map/all_gather | solution.py:189
  166.1 65.1 %reduce-scatter.11.cloned.1.call-start = ((), (), s32[]{:S(2)}) async-start(), calls=%async_computation.11 | async-start | bytes 1572864 | tf_op jit(solution)/shard_map/reduce_scatter | solution.py:209
  187.6 2.3 copy-start.5
  189.9 5.5 copy-start.3
  189.9 10.7 %slice-start = ((s8[8388608]{0:T(1024)(128)(4,1)}), s8[4194304]{0:T(1024)(128)(4,1)S(1)}, s32[]{:S(2)}) async-start(s8[8388608]{0:T(1024)(128)(4,1)} %bitcast.82), calls=%async_computation.15 | async-start | bytes 8388608
  195.4 5.2 slice-start.1
  205.5 2.5 copy-start.7
  210.8 43.7 %reduce-scatter.7.cloned.1.call-start = ((), (), s32[]{:S(2)}) async-start(), calls=%async_computation.7 | async-start | bytes 1572864 | tf_op jit(solution)/shard_map/reduce_scatter | solution.py:163
  215.8 211.8 %all-reduce.7.cloned.1.call-start = ((), (), s32[]{:S(2)}) async-start(), calls=%async_computation.12 | async-start | bytes 13631488 | tf_op jit(solution)/shard_map/psum | solution.py:225
  254.5 4.4 copy-start.13
  262.9 411.7 %all-reduce.11.cloned.1.call-start = ((), (), s32[]{:S(2)}) async-start(), calls=%async_computation.14 | async-start | bytes 25690112 | tf_op jit(solution)/shard_map/psum | solution.py:216
  283.2 5.0 copy-start.20
  283.2 5.1 copy-start.22
  293.6 531.8 %all-reduce.9.cloned.1.call-start = ((), (), s32[]{:S(2)}) async-start(), calls=%async_computation.13 | async-start | bytes 13631488 | tf_op jit(solution)/shard_map/psum | solution.py:224
  674.7 7.2 slice-start.2
  674.7 5.7 copy-start.12
  674.7 7.2 slice-start.3
  681.9 5.8 copy-start.8
  (8 other events, 10.0 us)
Sparse Core Ops, SparseCore 0:
  13.6 23.9 all-gather.6
  57.6 20.3 reduce-scatter.4
  82.0 21.3 all-gather.8
  104.8 21.2 all-gather.10
  140.8 20.3 reduce-scatter.8
  166.2 21.2 all-gather.12
  210.9 20.3 reduce-scatter.10
  234.1 20.3 reduce-scatter.6
  263.1 164.5 all-reduce.6
  433.9 240.7 all-reduce.10
  678.4 146.9 all-reduce.8
